TPU v7x, 256 devices: a whole 4x4x8 slice. The times are simulated.
256 devices in a mesh: dp: 64 (over y, z, core), tensor: 4 (over x).
Axes of the slice: x: 4, y: 4, z: 8, core: 2. Of those that a mesh axis runs over, the one named last changes fastest.
Arguments:
- activations: bfloat16 [32768, 8192], P('dp', 'tensor'), may hold values from -2000 to 2000
- norm_gain: float32 [8192], replicated, may hold values from 0.5 to 12
- w_query: bfloat16 [8192, 4096], P('dp', 'tensor'), may hold values from -0.0625 to 0.0625
- w_key: bfloat16 [8192, 512], P('dp', 'tensor'), may hold values from -0.0625 to 0.0625
- w_value: bfloat16 [8192, 512], P('dp', 'tensor'), may hold values from -0.0625 to 0.0625
- lengths: int32 [128], replicated, may hold values from 128 to 256
- languages: int32 [128], replicated, may hold values from 0 to 29
- lang_caps: int32 [30], replicated, may hold values from 128 to 256
- dest_shard: int32 [128], replicated, may hold values from 0 to 63, as said below
Outputs:
- attended: bfloat16 [32768, 4096], P('dp', 'tensor')
Inputs may be any that keep to these rules, and one draw needn't show every extreme that they name: `dest_shard`: every data shard receives exactly 2 documents.
All inputs are finite; a program needn't handle non-finite values.
Results may differ from a plain program's by a relative error of at most 0.007.
The roundings to bfloat16 on the way count: a program that leaves them out, or rounds other values in their place, can miss the bound.
Values may be sent and summed in bfloat16 or wider, within the bound.
A program may use at most 128 MiB of HBM per device.

v0:
```python
import math
import jax
import jax.numpy as jnp
from jax import lax
from jax.sharding import PartitionSpec as P

HEAD_WIDTH = 128
rope_base = 500000.0
norm_eps = 1e-05


def rotary_embedding(vectors, token_positions):
    half_width = vectors.shape[-1] // 2
    steps_range = jnp.arange(half_width, dtype=jnp.float32)
    frequency = jnp.exp(steps_range * (-2.0 * math.log(rope_base) / vectors.shape[-1]))
    angles = token_positions[..., None, None] * frequency
    cosine = jnp.cos(angles)
    sine_table = jnp.sin(angles)
    first_half = vectors[..., :half_width]
    second_half = vectors[..., half_width:]
    return jnp.concatenate(
        [
            first_half * cosine - second_half * sine_table,
            second_half * cosine + first_half * sine_table,
        ],
        axis=-1,
    )


def project(source_rows, norm_gain, w_query, w_key, w_value):
    gathered = lax.all_gather(source_rows, "tensor", axis=1, tiled=True)
    widened = gathered.astype(jnp.float32)
    row_scale = lax.rsqrt(jnp.mean(widened * widened, axis=1, keepdims=True) + norm_eps)
    normed = (widened * row_scale * norm_gain).astype(jnp.bfloat16)
    pieces = (
        lax.all_gather(w_query, "dp", axis=0, tiled=True),
        lax.all_gather(w_key, "dp", axis=0, tiled=True),
        lax.all_gather(w_value, "dp", axis=0, tiled=True),
    )
    return tuple(
        (
            jnp.dot(normed, weight_piece, preferred_element_type=jnp.float32)
            for weight_piece in pieces
        )
    )


def rotate_round(query_part, key_portion, value_portion, token_positions, head_dim):
    total_rows = query_part.shape[0]
    rotated_query = rotary_embedding(
        query_part.reshape(total_rows, -1, head_dim), token_positions
    ).reshape(total_rows, -1)
    rotated_key = rotary_embedding(
        key_portion.reshape(total_rows, -1, head_dim), token_positions
    ).reshape(total_rows, -1)
    return jnp.concatenate([rotated_query, rotated_key, value_portion], axis=1).astype(jnp.bfloat16)


def attend(packed, doc_lengths, query_width, key_width, head_dim, doc_max):
    total_rows = packed.shape[0]
    doc_total = total_rows // doc_max
    value_head_rows = key_width // head_dim
    heads_per_group = query_width // key_width
    queries = packed[:, :query_width].reshape(
        doc_total, doc_max, value_head_rows, heads_per_group, head_dim
    )
    key_rows = packed[:, query_width : query_width + key_width].reshape(
        doc_total, doc_max, value_head_rows, head_dim
    )
    value_rows = packed[:, query_width + key_width :].reshape(
        doc_total, doc_max, value_head_rows, head_dim
    )
    scores = jnp.einsum(
        "jqhgd,jkhd->jhgqk", queries, key_rows, preferred_element_type=jnp.float32
    ) / math.sqrt(head_dim)
    order_range = jnp.arange(doc_max)
    causal = order_range[:, None] >= order_range[None, :]
    scores = jnp.where(causal, scores, -jnp.inf)
    row_peak = jnp.max(scores, axis=-1, keepdims=True)
    exponent = jnp.exp(scores - row_peak)
    probability = (exponent / jnp.sum(exponent, axis=-1, keepdims=True)).astype(jnp.bfloat16)
    blended = jnp.einsum(
        "jhgqk,jkhd->jqhgd", probability, value_rows, preferred_element_type=jnp.float32
    )
    blended = blended.reshape(doc_total, doc_max, query_width)
    row_valid = order_range[None, :] < doc_lengths[:, None]
    result = jnp.where(row_valid[..., None], blended, 0.0)
    return result.reshape(total_rows, query_width).astype(jnp.bfloat16)


def local(
    activations, norm_gain, w_query, w_key, w_value, lengths, languages, lang_caps, dest_shard
):
    shard_count = lax.axis_size("dp")
    my_shard = lax.axis_index("dp")
    doc_count = lengths.shape[0]
    token_rows = activations.shape[0]
    rows_peer = token_rows // doc_count
    doc_max = rows_peer * shard_count
    docs_here = doc_count // shard_count
    head_dim = HEAD_WIDTH
    query_width = w_query.shape[1]
    key_width = w_key.shape[1]
    language_table = jnp.arange(lang_caps.shape[0])
    cap_of_doc = jnp.sum(
        jnp.where(languages[:, None] == language_table[None, :], lang_caps[None, :], 0), axis=1
    )
    capped = jnp.minimum(lengths, cap_of_doc)
    doc_order = jnp.arange(doc_count)
    same_dest = dest_shard[:, None] == dest_shard[None, :]
    doc_rank = jnp.sum(
        (same_dest & (doc_order[None, :] < doc_order[:, None])).astype(jnp.int32), axis=1
    )
    target_slot = dest_shard * docs_here + doc_rank
    holder = jnp.sum(
        jnp.where(doc_order[:, None] == target_slot[None, :], doc_order[None, :], 0), axis=1
    )
    mine = lax.dynamic_slice_in_dim(holder, my_shard * docs_here, docs_here)
    doc_lengths = jnp.take(capped, mine)
    holder_grid = jnp.transpose(holder.reshape(shard_count, docs_here))
    send_index = (
        holder_grid[:, None, :] * rows_peer + jnp.arange(rows_peer)[None, :, None]
    ).reshape(-1)
    outgoing = jnp.take(activations, send_index, axis=0).reshape(
        docs_here, rows_peer, shard_count, -1
    )
    arrived = lax.all_to_all(outgoing, "dp", split_axis=2, concat_axis=2, tiled=True)
    moved_rows = arrived.reshape(docs_here * doc_max, -1)
    query_part, key_portion, value_portion = project(moved_rows, norm_gain, w_query, w_key, w_value)
    token_positions = jnp.tile(jnp.arange(doc_max), docs_here).astype(jnp.float32)
    packed = rotate_round(query_part, key_portion, value_portion, token_positions, head_dim)
    return attend(packed, doc_lengths, query_width, key_width, head_dim, doc_max)


def solution(mesh):
    return jax.shard_map(
        local,
        mesh=mesh,
        in_specs=(
            P("dp", "tensor"),
            P(),
            P("dp", "tensor"),
            P("dp", "tensor"),
            P("dp", "tensor"),
            P(),
            P(),
            P(),
            P(),
        ),
        out_specs=P("dp", "tensor"),
        check_vma=False,
    )
```

profile of v0, /device:TPU:1, one launch (start us, length us, event | category | flops | bytes accessed | tf_op | source)
XLA Modules:
  0.0 453.7 jit_solution(18384676850716704676)
XLA Ops:
  6.5 0.0 copy-start
  6.5 0.0 all-gather.5.cloned.1.call-start
  6.5 1.0 convert_reduce_fusion
  7.5 0.7 multiply_add_fusion
  8.2 0.1 select_reduce_fusion
  8.3 0.1 mul.188
  8.5 0.1 copy.35
  8.6 0.1 add.84
  8.7 0.1 copy.36
  8.8 0.0 copy-done
  8.8 3.3 gather_fusion.1
  12.2 3.8 copy_select_fusion
  16.0 64.1 %all_to_all.5 = bf16[2,4,64,2048]{3,1,0,2:T(4,128)(2,1)S(1)} all-to-all(bf16[2,4,64,2048]{3,1,0,2:T(4,128)(2,1)S(1)} %copy_select_fusion), channel_id=1, replica_groups=mesh['dp'=64,'tensor'=4] {'dp'}, dimensions={2} | all-to-all | bytes 4194304 | tf_op jit(solution)/shard_map/all_to_all | solution.py:127
  80.1 2.5 copy.38
  82.7 0.0 all-gather.5.cloned.1.call-update
  82.7 0.0 all-gather.9.cloned.1.call-start
  82.7 0.7 all-gather.9.cloned.1.call-update
  83.4 0.0 all-gather.7.cloned.1.call-start
  83.5 0.7 all-gather.7.cloned.1.call-update
  84.2 0.0 all-gather.11.cloned.1.call-start
  84.2 0.5 all-gather.11.cloned.1.call-update
  84.8 0.0 copy-done.2
  84.8 0.0 copy-done.3
  84.8 0.1 select_reduce_fusion.1
  84.9 0.1 compare_select_fusion.2
  85.0 0.6 gather_fusion
  85.6 0.1 and_select_fusion
  85.7 0.1 iota_compare_fusion.4
  85.8 1.0 multiply_cosine_fusion
  86.8 0.0 copy-start.1
  86.8 77.9 %all-gather.5.cloned.1.call-done = bf16[512,8192]{1,0:T(8,128)(2,1)} async-done(((bf16[512,2048]{1,0:T(8,128)(2,1)}), bf16[512,8192]{1,0:T(8,128)(2,1)}) %all-gather.5.cloned.1.call-update) | async-done | bytes 8388624 | tf_op jit(solution)/shard_map/all_gather | solution.py:31
  164.7 5.1 %fusion = f32[512]{0:T(512)S(1)} fusion(bf16[512,8192]{1,0:T(8,128)(2,1)} %all-gather.5.cloned.1.call-done), kind=kLoop, calls=%fused_computation.4 | loop fusion | flops 12582400 | bytes 8390656 | tf_op jit(solution)/shard_map/reduce_sum | solution.py:33
  169.8 76.8 %all-gather.9.cloned.1.call-done = bf16[8192,128]{1,0:T(8,128)(2,1)} async-done(((bf16[128,128]{1,0:T(8,128)(2,1)}), bf16[8192,128]{1,0:T(8,128)(2,1)}) %all-gather.9.cloned.1.call-update) | async-done | bytes 2097168 | tf_op jit(solution)/shard_map/all_gather | solution.py:37
  246.6 6.5 %convolution_bitcast_fusion.1 = f32[512,1,128]{0,2,1:T(8,128)S(1)} fusion(bf16[8192,128]{1,0:T(8,128)(2,1)} %all-gather.9.cloned.1.call-done, bf16[512,8192]{1,0:T(8,128)(2,1)} %all-gather.5.cloned.1.call-done, f32[8192]{0:T(1024)S(1)} %copy-done.1, f32[512]{0:T(512)S(1)} %add_rsqrt_fusion), kind=kOutput, calls=%fused_computation.22 | convolution fusion | flops 1090519040 | bytes 10782720 | tf_op jit(solution)/shard_map/dot_general | solution.py:42
  253.1 0.6 fusion.19
  253.7 0.1 copy.49
  253.8 70.6 %all-gather.7.cloned.1.call-done = bf16[8192,128]{1,0:T(8,128)(2,1)} async-done(((bf16[128,128]{1,0:T(8,128)(2,1)}), bf16[8192,128]{1,0:T(8,128)(2,1)}) %all-gather.7.cloned.1.call-update) | async-done | bytes 2097168 | tf_op jit(solution)/shard_map/all_gather | solution.py:38
  324.4 6.4 %convolution_convert_fusion = bf16[512,128]{1,0:T(8,128)(2,1)S(1)} fusion(bf16[8192,128]{1,0:T(8,128)(2,1)} %all-gather.7.cloned.1.call-done, bf16[512,8192]{1,0:T(8,128)(2,1)} %all-gather.5.cloned.1.call-done, f32[8192]{0:T(1024)S(1)} %copy-done.1, f32[512]{0:T(512)S(1)} %add_rsqrt_fusion), kind=kOutput, calls=%fused_computation.23 | convolution fusion | flops 1090584576 | bytes 10651648 | tf_op jit(solution)/shard_map/dot_general | solution.py:42
  330.8 93.0 %all-gather.11.cloned.1.call-done = bf16[8192,1024]{1,0:T(8,128)(2,1)} async-done(((bf16[128,1024]{1,0:T(8,128)(2,1)}), bf16[8192,1024]{1,0:T(8,128)(2,1)}) %all-gather.11.cloned.1.call-update) | async-done | bytes 16777232 | tf_op jit(solution)/shard_map/all_gather | solution.py:36
  423.8 14.5 %convolution_bitcast_fusion = f32[64,8,8,128]{3,1,2,0:T(8,128)S(1)} fusion(bf16[8192,1024]{1,0:T(8,128)(2,1)} %all-gather.11.cloned.1.call-done, bf16[512,8192]{1,0:T(8,128)(2,1)} %all-gather.5.cloned.1.call-done, f32[8192]{0:T(1024)S(1)} %copy-done.1, f32[512]{0:T(512)S(1)} %add_rsqrt_fusion), kind=kOutput, calls=%fused_computation.21 | convolution fusion | flops 8606711808 | bytes 27297792 | tf_op jit(solution)/shard_map/dot_general | solution.py:42
  438.3 0.5 copy.51
  438.8 0.9 subtract_convert_fusion
  439.7 0.6 pad_maximum_fusion
  440.3 0.8 fusion.4
  441.0 0.9 fusion.3
  441.9 2.3 fusion.9
  444.2 1.7 copy.43
  445.9 1.2 fusion.5
  (19 shorter events, 0.2 us)
Async XLA Ops:
  6.5 2.3 copy-start
  6.5 158.2 %all-gather.5.cloned.1.call-start = ((), (), s32[]{:S(2)}) async-start(), calls=%async_computation.1 | async-start | bytes 10485760 | tf_op jit(solution)/shard_map/all_gather | solution.py:31
  80.1 4.6 %copy-start.2 = (s32[30]{0:T(128)S(1)}, s32[30]{0:T(128)}, u32[]{:S(2)}) copy-start(s32[30]{0:T(128)} %param.16) | copy-start | bytes 364
  80.1 4.6 %copy-start.3 = (s32[128]{0:T(128)S(1)}, s32[128]{0:T(128)}, u32[]{:S(2)}) copy-start(s32[128]{0:T(128)} %param.15) | copy-start | bytes 1540
  80.1 4.7 %copy-start.4 = (s32[128]{0:T(128)S(1)}, s32[128]{0:T(128)}, u32[]{:S(2)}) copy-start(s32[128]{0:T(128)} %param.14) | copy-start | bytes 1540
  82.7 164.0 %all-gather.9.cloned.1.call-start = ((), (), s32[]{:S(2)}) async-start(), calls=%async_computation.3 | async-start | bytes 2129920 | tf_op jit(solution)/shard_map/all_gather | solution.py:37
  83.4 241.0 %all-gather.7.cloned.1.call-start = ((), (), s32[]{:S(2)}) async-start(), calls=%async_computation.2 | async-start | bytes 2129920 | tf_op jit(solution)/shard_map/all_gather | solution.py:38
  84.2 339.6 %all-gather.11.cloned.1.call-start = ((), (), s32[]{:S(2)}) async-start(), calls=%async_computation.4 | async-start | bytes 17039360 | tf_op jit(solution)/shard_map/all_gather | solution.py:36
  86.8 159.8 %copy-start.1 = (f32[8192]{0:T(1024)S(1)}, f32[8192]{0:T(1024)}, u32[]{:S(2)}) copy-start(f32[8192]{0:T(1024)} %param.10) | copy-start | bytes 98308
Sparse Core Ops, SparseCore 0:
  82.8 81.8 all-gather.4
  167.5 79.0 all-gather.8
  249.4 74.9 all-gather.6
  327.1 96.6 all-gather.10
where the time goes:
time: 454 us
  waiting for transfers between devices  320 us (70%)
  blocking collectives  64.1 us (14%)
  matrix products  30.4 us (7%)
  other arithmetic  16.2 us (4%)
  between operations  13.3 us (3%)
  local copies, waits for them, and re-layouts  9.25 us (2%)
    all_gather x1, waiting for transfers between devices, project(): lax.all_gather(w_query, 'dp', axis=0, tiled=True)  93 us
    all_gather x1, waiting for transfers between devices, project(): gathered = lax.all_gather(source_rows, 'tensor', axis=1, tiled=True)  77.9 us
    all_gather x1, waiting for transfers between devices, project(): lax.all_gather(w_key, 'dp', axis=0, tiled=True)  76.8 us
    all_gather x1, waiting for transfers between devices, project(): lax.all_gather(w_value, 'dp', axis=0, tiled=True)  70.6 us
    all_to_all x1, blocking collectives, local(): lax.all_to_all(outgoing, 'dp', split_axis=2, concat_axis=2, tiled=True)  64.1 us
    dot_general x3, matrix products, project(): jnp.dot(normed, weight_piece, preferred_element_type=jnp.float32)  27.4 us
  transfers between devices with their start and end apart: 4, of which 4 were waited for; matrix products, arithmetic and copies ran while one was open for 5% of the time, Pallas kernels for 0%

commit v1 on v0

--- a/solution.py
+++ b/solution.py
@@ -34,7 +34,9 @@
     normed = (widened * row_scale * norm_gain).astype(jnp.bfloat16)
     pieces = (
         lax.all_gather(w_query, "dp", axis=0, tiled=True),
-        lax.all_gather(w_key, "dp", axis=0, tiled=True),
+        jnp.concatenate(
+            lax.all_to_all(jnp.stack([w_key] * lax.axis_size("dp")), "dp", 0, 0), axis=0
+        ),
         lax.all_gather(w_value, "dp", axis=0, tiled=True),
     )
     return tuple(

time: 454 us -> 376 us (0.83)
  waiting for transfers between devices: 320 us -> 235 us
  starting transfers between devices: 0.12 us -> 6.11 us
    all_gather x1 -> x0, waiting for transfers between devices: 76.8 us -> none  [project(): lax.all_gather(w_key, 'dp', axis=0, tiled=True)]
    all_gather x1, waiting for transfers between devices: 77.9 us -> 70.6 us  [project(): gathered = lax.all_gather(source_rows, 'tensor', axis=1, tiled=True)]
    all_to_all x0 -> x1, starting transfers between devices: none -> 6.03 us  [project(): lax.all_to_all(jnp.stack([w_key] * lax.axis_size('dp')), 'dp', 0, 0)]
  transfers between devices with their start and end apart: 4 -> 4, of which waited for: 4 -> 3; matrix products, arithmetic and copies ran while one was open for 5% -> 6% of each run, Pallas kernels for 0% -> 0%
where the time goes in v1:
time: 376 us
  waiting for transfers between devices  235 us (62%)
  blocking collectives  64.1 us (17%)
  matrix products  30.6 us (8%)
  other arithmetic  16.2 us (4%)
  between operations  13.3 us (4%)
  local copies, waits for them, and re-layouts  11 us (3%)
  starting transfers between devices  6.11 us (2%)
    all_gather x1, waiting for transfers between devices, project(): lax.all_gather(w_query, 'dp', axis=0, tiled=True)  93.1 us
    all_gather x1, waiting for transfers between devices, project(): gathered = lax.all_gather(source_rows, 'tensor', axis=1, tiled=True)  70.6 us
    all_gather x1, waiting for transfers between devices, project(): lax.all_gather(w_value, 'dp', axis=0, tiled=True)  69.6 us
    all_to_all x1, blocking collectives, local(): lax.all_to_all(outgoing, 'dp', split_axis=2, concat_axis=2, tiled=True)  64.1 us
    dot_general x3, matrix products, project(): jnp.dot(normed, weight_piece, preferred_element_type=jnp.float32)  27.6 us
  transfers between devices with their start and end apart: 4, of which 3 were waited for; matrix products, arithmetic and copies ran while one was open for 6% of the time, Pallas kernels for 0%

profile of v1, /device:TPU:1, one launch (start us, length us, event | category | flops | bytes accessed | tf_op | source)
XLA Modules:
  0.0 376.2 jit_solution(10887657832484510054)
XLA Ops:
  6.5 0.0 copy-start
  6.5 1.0 convert_reduce_fusion
  7.5 0.7 multiply_add_fusion
  8.2 0.1 select_reduce_fusion
  8.3 0.1 mul.188
  8.5 0.1 copy.35
  8.6 0.1 add.84
  8.7 0.1 copy.36
  8.8 3.3 gather_fusion.1
  12.2 3.8 %copy_select_fusion = bf16[2,4,64,2048]{3,1,0,2:T(4,128)(2,1)S(1)} fusion(bf16[2,4,64,2048]{3,2,1,0:T(8,128)(2,1)} %bitcast.61, pred[2,4,64]{1,0,2:T(4,128)(4,1)S(1)} %copy.36), kind=kLoop, calls=%fused_computation.16 | loop fusion | flops 1048576 | bytes 4194816 | tf_op jit(solution)/shard_map/jit(_take)/select_n | solution.py:126
  16.0 64.1 %all_to_all.10 = bf16[2,4,64,2048]{3,1,0,2:T(4,128)(2,1)S(1)} all-to-all(bf16[2,4,64,2048]{3,1,0,2:T(4,128)(2,1)S(1)} %copy_select_fusion), channel_id=1, replica_groups=mesh['dp'=64,'tensor'=4] {'dp'}, dimensions={2} | all-to-all | bytes 4194304 | tf_op jit(solution)/shard_map/all_to_all | solution.py:129
  80.1 2.5 copy.38
  82.6 0.0 all-gather.4.cloned.1.call-update
  82.6 0.0 all-gather.6.cloned.1.call-start
  82.7 0.7 all-gather.6.cloned.1.call-update
  83.4 0.0 all-gather.8.cloned.1.call-start
  83.4 0.7 all-gather.8.cloned.1.call-update
  84.1 0.0 copy-done.1
  84.1 1.8 stack.2
  86.0 6.0 %all-to-all-start.1 = ((bf16[64,128,128]{2,1,0:T(8,128)(2,1)}), bf16[64,128,128]{2,1,0:T(8,128)(2,1)}, u32[]{:S(2)}, u32[]{:S(2)}) async-start(bf16[64,128,128]{2,1,0:T(8,128)(2,1)} %stack.2), calls=%async_computation.1 | async-start | bytes 4194304 | tf_op jit(solution)/shard_map/all_to_all | solution.py:38
  92.0 0.0 copy-done.3
  92.0 0.0 copy-done.4
  92.0 0.1 select_reduce_fusion.1
  92.1 0.0 copy-done.5
  92.1 0.1 compare_select_fusion.2
  92.2 0.6 gather_fusion
  92.9 0.1 and_select_fusion
  93.0 0.1 iota_compare_fusion.4
  93.1 1.0 multiply_cosine_fusion
  94.1 0.0 copy-start.2
  94.1 70.6 %all-gather.4.cloned.1.call-done = bf16[512,8192]{1,0:T(8,128)(2,1)} async-done(((bf16[512,2048]{1,0:T(8,128)(2,1)}), bf16[512,8192]{1,0:T(8,128)(2,1)}) %all-gather.4.cloned.1.call-update) | async-done | bytes 8388624 | tf_op jit(solution)/shard_map/all_gather | solution.py:31
  164.7 5.1 %fusion = f32[512]{0:T(512)S(1)} fusion(bf16[512,8192]{1,0:T(8,128)(2,1)} %all-gather.4.cloned.1.call-done), kind=kLoop, calls=%fused_computation.4 | loop fusion | flops 12582400 | bytes 8390656 | tf_op jit(solution)/shard_map/reduce_sum | solution.py:33
  169.8 0.0 all-to-all-done.1
  169.8 6.5 %convolution_bitcast_fusion.1 = f32[512,1,128]{0,2,1:T(8,128)S(1)} fusion(bf16[8192,128]{1,0:T(8,128)(2,1)} %bitcast.6, bf16[512,8192]{1,0:T(8,128)(2,1)} %all-gather.4.cloned.1.call-done, f32[8192]{0:T(1024)S(1)} %copy-done.2, f32[512]{0:T(512)S(1)} %add_rsqrt_fusion), kind=kOutput, calls=%fused_computation.22 | convolution fusion | flops 1090519040 | bytes 10782720 | tf_op jit(solution)/shard_map/dot_general | solution.py:44
  176.3 0.6 fusion.19
  176.9 0.1 copy.49
  177.0 69.6 %all-gather.6.cloned.1.call-done = bf16[8192,128]{1,0:T(8,128)(2,1)} async-done(((bf16[128,128]{1,0:T(8,128)(2,1)}), bf16[8192,128]{1,0:T(8,128)(2,1)}) %all-gather.6.cloned.1.call-update) | async-done | bytes 2097168 | tf_op jit(solution)/shard_map/all_gather | solution.py:40
  246.6 6.4 %convolution_convert_fusion = bf16[512,128]{1,0:T(8,128)(2,1)S(1)} fusion(bf16[8192,128]{1,0:T(8,128)(2,1)} %all-gather.6.cloned.1.call-done, bf16[512,8192]{1,0:T(8,128)(2,1)} %all-gather.4.cloned.1.call-done, f32[8192]{0:T(1024)S(1)} %copy-done.2, f32[512]{0:T(512)S(1)} %add_rsqrt_fusion), kind=kOutput, calls=%fused_computation.23 | convolution fusion | flops 1090584576 | bytes 10651648 | tf_op jit(solution)/shard_map/dot_general | solution.py:44
  253.0 93.1 %all-gather.8.cloned.1.call-done = bf16[8192,1024]{1,0:T(8,128)(2,1)} async-done(((bf16[128,1024]{1,0:T(8,128)(2,1)}), bf16[8192,1024]{1,0:T(8,128)(2,1)}) %all-gather.8.cloned.1.call-update) | async-done | bytes 16777232 | tf_op jit(solution)/shard_map/all_gather | solution.py:36
  346.1 14.7 %convolution_bitcast_fusion = f32[64,8,8,128]{3,1,2,0:T(8,128)S(1)} fusion(bf16[8192,1024]{1,0:T(8,128)(2,1)} %all-gather.8.cloned.1.call-done, bf16[512,8192]{1,0:T(8,128)(2,1)} %all-gather.4.cloned.1.call-done, f32[8192]{0:T(1024)S(1)} %copy-done.2, f32[512]{0:T(512)S(1)} %add_rsqrt_fusion), kind=kOutput, calls=%fused_computation.21 | convolution fusion | flops 8606711808 | bytes 27297792 | tf_op jit(solution)/shard_map/dot_general | solution.py:44
  360.9 0.5 copy.51
  361.3 0.9 subtract_convert_fusion
  362.2 0.6 pad_maximum_fusion
  362.8 0.8 fusion.4
  363.6 0.9 fusion.3
  364.4 2.3 fusion.9
  366.7 1.7 copy.43
  368.4 1.2 fusion.5
  (21 shorter events, 0.2 us)
Async XLA Ops:
  6.5 2.3 copy-start
  6.5 158.2 %all-gather.4.cloned.1.call-start = ((), (), s32[]{:S(2)}) async-start(), calls=%async_computation.2 | async-start | bytes 10485760 | tf_op jit(solution)/shard_map/all_gather | solution.py:31
  80.1 4.0 %copy-start.1 = (bf16[128,128]{1,0:T(8,128)(2,1)S(1)}, bf16[128,128]{1,0:T(8,128)(2,1)}, u32[]{:S(2)}) copy-start(bf16[128,128]{1,0:T(8,128)(2,1)} %param.12) | copy-start | bytes 98308
  82.6 9.4 %copy-start.3 = (s32[30]{0:T(128)S(1)}, s32[30]{0:T(128)}, u32[]{:S(2)}) copy-start(s32[30]{0:T(128)} %param.16) | copy-start | bytes 364
  82.6 9.4 %copy-start.4 = (s32[128]{0:T(128)S(1)}, s32[128]{0:T(128)}, u32[]{:S(2)}) copy-start(s32[128]{0:T(128)} %param.15) | copy-start | bytes 1540
  82.6 9.5 %copy-start.5 = (s32[128]{0:T(128)S(1)}, s32[128]{0:T(128)}, u32[]{:S(2)}) copy-start(s32[128]{0:T(128)} %param.14) | copy-start | bytes 1540
  82.6 164.0 %all-gather.6.cloned.1.call-start = ((), (), s32[]{:S(2)}) async-start(), calls=%async_computation.3 | async-start | bytes 2129920 | tf_op jit(solution)/shard_map/all_gather | solution.py:40
  83.4 262.7 %all-gather.8.cloned.1.call-start = ((), (), s32[]{:S(2)}) async-start(), calls=%async_computation.4 | async-start | bytes 17039360 | tf_op jit(solution)/shard_map/all_gather | solution.py:36
  86.0 83.9 %all-to-all-start.1 = ((bf16[64,128,128]{2,1,0:T(8,128)(2,1)}), bf16[64,128,128]{2,1,0:T(8,128)(2,1)}, u32[]{:S(2)}, u32[]{:S(2)}) async-start(bf16[64,128,128]{2,1,0:T(8,128)(2,1)} %stack.2), calls=%async_computation.1 | async-start | bytes 4194304 | tf_op jit(solution)/shard_map/all_to_all | solution.py:38
  94.1 75.7 %copy-start.2 = (f32[8192]{0:T(1024)S(1)}, f32[8192]{0:T(1024)}, u32[]{:S(2)}) copy-start(f32[8192]{0:T(1024)} %param.10) | copy-start | bytes 98308
Sparse Core Ops, SparseCore 0:
  82.8 81.8 all-gather.3
  167.5 79.0 all-gather.5
  249.4 96.6 all-gather.7
